TPU v7x, 256 devices: a whole 4x4x8 slice. The times are simulated.
256 devices in a mesh: prow: 32 (over y, z), pcol: 8 (over x, core).
Axes of the slice: x: 4, y: 4, z: 8, core: 2. Of those that a mesh axis runs over, the one named last changes fastest.
Arguments:
- right_side: bfloat16 [32, 6, 128, 256], P('prow'), may hold values from -6 to 6
- lower_inverse: bfloat16 [32, 6, 256, 256], P('prow'), as said below
- upper_inverse: bfloat16 [32, 6, 256, 256], P('prow'), as said below
- lower_blocks: bfloat16 [32, 5, 48, 256, 256], P('prow', None, 'pcol'), may hold values from -0.0546875 to 0.0546875
- lower_sources: int32 [32, 5, 48], P('prow', None, 'pcol'), may hold values from 0 to 159, as said below
- lower_counts: int32 [32, 5, 8], P('prow', None, 'pcol'), may hold values from 1 to 6, as said below
- upper_blocks: bfloat16 [32, 5, 48, 256, 256], P('prow', None, 'pcol'), may hold values from -0.0546875 to 0.0546875
- upper_sources: int32 [32, 5, 48], P('prow', None, 'pcol'), may hold values from 32 to 191, as said below
- upper_counts: int32 [32, 5, 8], P('prow', None, 'pcol'), may hold values from 1 to 6, as said below
Outputs:
- solution: bfloat16 [32, 6, 128, 256], P('prow')
Inputs may be any that keep to these rules, and one draw needn't show every extreme that they name: `lower_sources`: entry [r, l, c] names supernode v * 32 + p of a level v below l + 1, with p % (8) == c // 6; entries may repeat. `upper_sources`: entry [r, l, c] names supernode v * 32 + p of a level v above l, with p % (8) == c // 6; entries may repeat. `lower_counts`: entry [r, l, g] is how many of the 6 slots of group g are live; the live ones come first. `upper_counts`: entry [r, l, g] is how many of the 6 slots of group g are live; the live ones come first. `lower_inverse`: each block is lower triangular. `upper_inverse`: each block is upper triangular.
All inputs are finite; a program needn't handle non-finite values.
Results may differ from a plain program's by a relative error of at most 0.02.
Values may be sent and summed in bfloat16 or wider, within the bound.
No kernel may reach another device: no remote copies, remote signals or barrier semaphores. Data moves between devices by JAX's collectives and lax.ppermute only.
A program may use at most 64 MiB of HBM per device.

v0:
```python
import jax
import jax.numpy as jnp
from jax import lax
from jax.sharding import PartitionSpec as P


def pick_sources(sources, count, store, width, ncol):
    group = store.shape[1]
    flat = store.reshape(store.shape[0] * group, store.shape[2], store.shape[3])
    position = sources // width * group + sources % width // ncol
    picked = flat[position]
    live = jnp.arange(sources.shape[0], dtype=jnp.int32) < count
    return jnp.where(live[:, None, None], picked, jnp.zeros_like(picked))


def contract(picked, blocks):
    return lax.dot_general(
        picked, blocks, (((0, 2), (0, 2)), ((), ())), preferred_element_type=jnp.float32
    )


def apply_inverse(residual, inverse):
    product = lax.dot_general(
        residual, inverse, (((1,), (1,)), ((), ())), preferred_element_type=jnp.float32
    )
    return product.astype(jnp.bfloat16)


def solve_level(right, inverse, blocks, sources, count, store):
    width = lax.axis_size("prow")
    ncol = lax.axis_size("pcol")
    picked = pick_sources(sources, count, store, width, ncol)
    total = lax.psum(contract(picked, blocks), "pcol")
    residual = (right.astype(jnp.float32) - total).astype(jnp.bfloat16)
    return apply_inverse(residual, inverse)


def spread(solved):
    ncol = lax.axis_size("pcol")
    column = lax.axis_index("pcol")
    whole = lax.all_gather(solved[None], "prow", axis=0, tiled=True)
    whole = whole.reshape(whole.shape[0] // ncol, ncol, whole.shape[1], whole.shape[2])
    return lax.dynamic_index_in_dim(whole, column, 1, keepdims=False)


def shards(
    right_side,
    lower_inverse,
    upper_inverse,
    lower_blocks,
    lower_sources,
    lower_counts,
    upper_blocks,
    upper_sources,
    upper_counts,
):
    group = lax.axis_size("prow") // lax.axis_size("pcol")
    levels = right_side.shape[1]
    shape = (levels, group, right_side.shape[2], right_side.shape[3])
    forward_store = jnp.zeros(shape, jnp.bfloat16)
    forward_own = []
    for level in range(levels):
        if level == 0:
            solved = apply_inverse(right_side[0, 0], lower_inverse[0, 0])
        else:
            solved = solve_level(
                right_side[0, level],
                lower_inverse[0, level],
                lower_blocks[0, level - 1],
                lower_sources[0, level - 1],
                lower_counts[0, level - 1, 0],
                forward_store,
            )
        forward_own.append(solved)
        if level + 1 < levels:
            forward_store = forward_store.at[level].set(spread(solved))
    backward_store = jnp.zeros(shape, jnp.bfloat16)
    backward_own = [None] * levels
    for level in range(levels - 1, -1, -1):
        if level == levels - 1:
            solved = apply_inverse(forward_own[level], upper_inverse[0, level])
        else:
            solved = solve_level(
                forward_own[level],
                upper_inverse[0, level],
                upper_blocks[0, level],
                upper_sources[0, level],
                upper_counts[0, level, 0],
                backward_store,
            )
        backward_own[level] = solved
        if level > 0:
            backward_store = backward_store.at[level].set(spread(solved))
    return jnp.stack(backward_own)[None]


def solution(mesh):
    in_specs = (
        P("prow", None, None, None),
        P("prow", None, None, None),
        P("prow", None, None, None),
        P("prow", None, "pcol", None, None),
        P("prow", None, "pcol"),
        P("prow", None, "pcol"),
        P("prow", None, "pcol", None, None),
        P("prow", None, "pcol"),
        P("prow", None, "pcol"),
    )
    out_specs = P("prow", None, None, None)
    return jax.shard_map(shards, mesh=mesh, in_specs=in_specs, out_specs=out_specs, check_vma=False)
```

profile of v0, /device:TPU:8, one launch (start us, length us, event | category | flops | bytes accessed | tf_op | source)
XLA Modules:
  0.0 1472.5 jit_solution(6980355928719453003)
XLA Ops:
  6.5 1.8 convolution_convert_fusion.11
  8.4 1.5 fusion.124
  10.6 1.4 fusion.107
  12.0 77.6 %all-gather.21.cloned.1.call-done = bf16[4096,256]{1,0:T(8,128)(2,1)} async-done(((bf16[128,256]{1,0:T(8,128)(2,1)}), bf16[4096,256]{1,0:T(8,128)(2,1)}) %all-gather.21.cloned.1.call-update) | async-done | bytes 2097168 | tf_op jit(solution)/shard_map/all_gather | solution.py:41
  91.3 2.2 convolution_bitcast_fusion.9
  93.6 62.8 %all-reduce.13.cloned.1.call-done = f32[128,256]{1,0:T(8,128)} async-done(((f32[128,256]{1,0:T(8,128)}), f32[128,256]{1,0:T(8,128)}) %all-reduce.13.cloned.1.call-update) | async-done | bytes 131088 | tf_op jit(solution)/shard_map/psum | solution.py:33
  156.4 1.7 convolution_convert_fusion.10
  159.0 76.3 %all-gather.23.cloned.1.call-done = bf16[4096,256]{1,0:T(8,128)(2,1)} async-done(((bf16[128,256]{1,0:T(8,128)(2,1)}), bf16[4096,256]{1,0:T(8,128)(2,1)}) %all-gather.23.cloned.1.call-update) | async-done | bytes 2097168 | tf_op jit(solution)/shard_map/all_gather | solution.py:41
  235.2 1.0 bitcast_dynamic-update-slice_fusion.7
  236.8 2.2 convolution_bitcast_fusion.8
  239.1 62.8 %all-reduce.15.cloned.1.call-done = f32[128,256]{1,0:T(8,128)} async-done(((f32[128,256]{1,0:T(8,128)}), f32[128,256]{1,0:T(8,128)}) %all-reduce.15.cloned.1.call-update) | async-done | bytes 131088 | tf_op jit(solution)/shard_map/psum | solution.py:33
  301.9 1.7 convolution_convert_fusion.9
  304.4 75.8 %all-gather.25.cloned.1.call-done = bf16[4096,256]{1,0:T(8,128)(2,1)} async-done(((bf16[128,256]{1,0:T(8,128)(2,1)}), bf16[4096,256]{1,0:T(8,128)(2,1)}) %all-gather.25.cloned.1.call-update) | async-done | bytes 2097168 | tf_op jit(solution)/shard_map/all_gather | solution.py:41
  380.2 1.0 bitcast_dynamic-update-slice_fusion.6
  381.7 2.2 convolution_bitcast_fusion.7
  384.0 62.8 %all-reduce.17.cloned.1.call-done = f32[128,256]{1,0:T(8,128)} async-done(((f32[128,256]{1,0:T(8,128)}), f32[128,256]{1,0:T(8,128)}) %all-reduce.17.cloned.1.call-update) | async-done | bytes 131088 | tf_op jit(solution)/shard_map/psum | solution.py:33
  446.8 1.7 convolution_convert_fusion.8
  449.3 76.3 %all-gather.27.cloned.1.call-done = bf16[4096,256]{1,0:T(8,128)(2,1)} async-done(((bf16[128,256]{1,0:T(8,128)(2,1)}), bf16[4096,256]{1,0:T(8,128)(2,1)}) %all-gather.27.cloned.1.call-update) | async-done | bytes 2097168 | tf_op jit(solution)/shard_map/all_gather | solution.py:41
  527.2 2.2 convolution_bitcast_fusion.6
  529.4 62.8 %all-reduce.19.cloned.1.call-done = f32[128,256]{1,0:T(8,128)} async-done(((f32[128,256]{1,0:T(8,128)}), f32[128,256]{1,0:T(8,128)}) %all-reduce.19.cloned.1.call-update) | async-done | bytes 131088 | tf_op jit(solution)/shard_map/psum | solution.py:33
  592.2 1.7 convolution_convert_fusion.7
  594.0 1.1 iota_compare_fusion.8
  595.8 74.9 %all-gather.29.cloned.1.call-done = bf16[4096,256]{1,0:T(8,128)(2,1)} async-done(((bf16[128,256]{1,0:T(8,128)(2,1)}), bf16[4096,256]{1,0:T(8,128)(2,1)}) %all-gather.29.cloned.1.call-update) | async-done | bytes 2097168 | tf_op jit(solution)/shard_map/all_gather | solution.py:41
  672.3 2.2 convolution_bitcast_fusion.5
  674.5 62.8 %all-reduce.21.cloned.1.call-done = f32[128,256]{1,0:T(8,128)} async-done(((f32[128,256]{1,0:T(8,128)}), f32[128,256]{1,0:T(8,128)}) %all-reduce.21.cloned.1.call-update) | async-done | bytes 131088 | tf_op jit(solution)/shard_map/psum | solution.py:33
  737.4 1.9 convolution_convert_fusion.5
  741.3 74.9 %all-gather.31.cloned.1.call-done = bf16[4096,256]{1,0:T(8,128)(2,1)} async-done(((bf16[128,256]{1,0:T(8,128)(2,1)}), bf16[4096,256]{1,0:T(8,128)(2,1)}) %all-gather.31.cloned.1.call-update) | async-done | bytes 2097168 | tf_op jit(solution)/shard_map/all_gather | solution.py:41
  817.9 2.2 convolution_bitcast_fusion.4
  820.2 62.8 %all-reduce.23.cloned.1.call-done = f32[128,256]{1,0:T(8,128)} async-done(((f32[128,256]{1,0:T(8,128)}), f32[128,256]{1,0:T(8,128)}) %all-reduce.23.cloned.1.call-update) | async-done | bytes 131088 | tf_op jit(solution)/shard_map/psum | solution.py:33
  883.0 1.7 convolution_convert_fusion.4
  885.5 75.9 %all-gather.33.cloned.1.call-done = bf16[4096,256]{1,0:T(8,128)(2,1)} async-done(((bf16[128,256]{1,0:T(8,128)(2,1)}), bf16[4096,256]{1,0:T(8,128)(2,1)}) %all-gather.33.cloned.1.call-update) | async-done | bytes 2097168 | tf_op jit(solution)/shard_map/all_gather | solution.py:41
  961.4 1.0 bitcast_dynamic-update-slice_fusion.3
  963.0 2.2 convolution_bitcast_fusion.3
  965.3 62.8 %all-reduce.25.cloned.1.call-done = f32[128,256]{1,0:T(8,128)} async-done(((f32[128,256]{1,0:T(8,128)}), f32[128,256]{1,0:T(8,128)}) %all-reduce.25.cloned.1.call-update) | async-done | bytes 131088 | tf_op jit(solution)/shard_map/psum | solution.py:33
  1028.1 1.7 convolution_convert_fusion.3
  1030.5 76.2 %all-gather.35.cloned.1.call-done = bf16[4096,256]{1,0:T(8,128)(2,1)} async-done(((bf16[128,256]{1,0:T(8,128)(2,1)}), bf16[4096,256]{1,0:T(8,128)(2,1)}) %all-gather.35.cloned.1.call-update) | async-done | bytes 2097168 | tf_op jit(solution)/shard_map/all_gather | solution.py:41
  1106.7 1.0 bitcast_dynamic-update-slice_fusion.2
  1108.3 2.2 convolution_bitcast_fusion.2
  1110.6 62.8 %all-reduce.27.cloned.1.call-done = f32[128,256]{1,0:T(8,128)} async-done(((f32[128,256]{1,0:T(8,128)}), f32[128,256]{1,0:T(8,128)}) %all-reduce.27.cloned.1.call-update) | async-done | bytes 131088 | tf_op jit(solution)/shard_map/psum | solution.py:33
  1173.4 1.7 convolution_convert_fusion.2
  1175.8 75.9 %all-gather.37.cloned.1.call-done = bf16[4096,256]{1,0:T(8,128)(2,1)} async-done(((bf16[128,256]{1,0:T(8,128)(2,1)}), bf16[4096,256]{1,0:T(8,128)(2,1)}) %all-gather.37.cloned.1.call-update) | async-done | bytes 2097168 | tf_op jit(solution)/shard_map/all_gather | solution.py:41
  1253.2 2.2 convolution_bitcast_fusion.1
  1255.5 62.8 %all-reduce.29.cloned.1.call-done = f32[128,256]{1,0:T(8,128)} async-done(((f32[128,256]{1,0:T(8,128)}), f32[128,256]{1,0:T(8,128)}) %all-reduce.29.cloned.1.call-update) | async-done | bytes 131088 | tf_op jit(solution)/shard_map/psum | solution.py:33
  1318.3 1.7 convolution_convert_fusion.1
  1320.8 76.3 %all-gather.39.cloned.1.call-done = bf16[4096,256]{1,0:T(8,128)(2,1)} async-done(((bf16[128,256]{1,0:T(8,128)(2,1)}), bf16[4096,256]{1,0:T(8,128)(2,1)}) %all-gather.39.cloned.1.call-update) | async-done | bytes 2097168 | tf_op jit(solution)/shard_map/all_gather | solution.py:41
  1398.7 2.2 convolution_bitcast_fusion
  1400.9 62.8 %all-reduce.31.cloned.1.call-done = f32[128,256]{1,0:T(8,128)} async-done(((f32[128,256]{1,0:T(8,128)}), f32[128,256]{1,0:T(8,128)}) %all-reduce.31.cloned.1.call-update) | async-done | bytes 131088 | tf_op jit(solution)/shard_map/psum | solution.py:33
  1463.7 1.1 fusion.1
  (117 shorter events, 21.7 us)
Async XLA Ops:
  6.5 83.1 %all-gather.21.cloned.1.call-start = ((), (), s32[]{:S(2)}) async-start(), calls=%async_computation.10 | async-start | bytes 2162688 | tf_op jit(solution)/shard_map/all_gather | solution.py:41
  8.3 148.1 %all-reduce.13.cloned.1.call-start = ((), (), s32[]{:S(2)}) async-start(), calls=%async_computation | async-start | bytes 262144 | tf_op jit(solution)/shard_map/psum | solution.py:33
  90.6 65.9 %copy-start.1 = (bf16[1,6,256,256]{3,2,1,0:T(8,128)(2,1)S(1)}, bf16[1,6,256,256]{3,2,1,0:T(8,128)(2,1)}, u32[]{:S(2)}) copy-start(bf16[1,6,256,256]{3,2,1,0:T(8,128)(2,1)} %param.30) | copy-start | bytes 2359300
  90.6 65.8 %copy-start.12 = (bf16[1,6,128,256]{3,2,1,0:T(8,128)(2,1)S(1)}, bf16[1,6,128,256]{3,2,1,0:T(8,128)(2,1)}, u32[]{:S(2)}) copy-start(bf16[1,6,128,256]{3,2,1,0:T(8,128)(2,1)} %param.29) | copy-start | bytes 1179652
  93.6 141.7 %all-gather.23.cloned.1.call-start = ((), (), s32[]{:S(2)}) async-start(), calls=%async_computation.11 | async-start | bytes 2162688 | tf_op jit(solution)/shard_map/all_gather | solution.py:41
  158.2 143.7 %all-reduce.15.cloned.1.call-start = ((), (), s32[]{:S(2)}) async-start(), calls=%async_computation.1 | async-start | bytes 262144 | tf_op jit(solution)/shard_map/psum | solution.py:33
  239.0 141.2 %all-gather.25.cloned.1.call-start = ((), (), s32[]{:S(2)}) async-start(), calls=%async_computation.12 | async-start | bytes 2162688 | tf_op jit(solution)/shard_map/all_gather | solution.py:41
  303.6 143.2 %all-reduce.17.cloned.1.call-start = ((), (), s32[]{:S(2)}) async-start(), calls=%async_computation.2 | async-start | bytes 262144 | tf_op jit(solution)/shard_map/psum | solution.py:33
  383.9 141.7 %all-gather.27.cloned.1.call-start = ((), (), s32[]{:S(2)}) async-start(), calls=%async_computation.13 | async-start | bytes 2162688 | tf_op jit(solution)/shard_map/all_gather | solution.py:41
  448.6 143.7 %all-reduce.19.cloned.1.call-start = ((), (), s32[]{:S(2)}) async-start(), calls=%async_computation.3 | async-start | bytes 262144 | tf_op jit(solution)/shard_map/psum | solution.py:33
  529.3 208.0 %copy-start = (bf16[1,6,256,256]{3,2,1,0:T(8,128)(2,1)S(1)}, bf16[1,6,256,256]{3,2,1,0:T(8,128)(2,1)}, u32[]{:S(2)}) copy-start(bf16[1,6,256,256]{3,2,1,0:T(8,128)(2,1)} %param.31) | copy-start | bytes 2359300
  529.4 209.9 %copy-start.13 = (s32[1,5,1]{1,2,0:T(1,128)S(1)}, s32[1,5,1]{1,2,0:T(1,128)}, u32[]{:S(2)}) copy-start(s32[1,5,1]{1,2,0:T(1,128)} %param.37) | copy-start | bytes 64
  529.4 141.3 %all-gather.29.cloned.1.call-start = ((), (), s32[]{:S(2)}) async-start(), calls=%async_computation.14 | async-start | bytes 2162688 | tf_op jit(solution)/shard_map/all_gather | solution.py:41
  594.0 143.4 %all-reduce.21.cloned.1.call-start = ((), (), s32[]{:S(2)}) async-start(), calls=%async_computation.4 | async-start | bytes 262144 | tf_op jit(solution)/shard_map/psum | solution.py:33
  674.5 141.7 %all-gather.31.cloned.1.call-start = ((), (), s32[]{:S(2)}) async-start(), calls=%async_computation.15 | async-start | bytes 2162688 | tf_op jit(solution)/shard_map/all_gather | solution.py:41
  739.2 143.7 %all-reduce.23.cloned.1.call-start = ((), (), s32[]{:S(2)}) async-start(), calls=%async_computation.5 | async-start | bytes 262144 | tf_op jit(solution)/shard_map/psum | solution.py:33
  817.1 65.9 %copy-start.10 = (bf16[128,256]{1,0:T(8,128)(2,1)S(1)}, bf16[128,256]{1,0:T(8,128)(2,1)}, u32[]{:S(2)}) copy-start(bf16[128,256]{1,0:T(8,128)(2,1)} %convolution_convert_fusion.7) | copy-start | bytes 196612
  817.1 68.3 %copy-start.16 = (s32[6]{0:T(128)S(1)}, s32[6]{0:T(128)}, u32[]{:S(2)}) copy-start(s32[6]{0:T(128)} %get-tuple-element.147) | copy-start | bytes 76
  820.1 208.0 %copy-start.9 = (bf16[128,256]{1,0:T(8,128)(2,1)S(1)}, bf16[128,256]{1,0:T(8,128)(2,1)}, u32[]{:S(2)}) copy-start(bf16[128,256]{1,0:T(8,128)(2,1)} %convolution_convert_fusion.8) | copy-start | bytes 196612
  820.1 210.4 %copy-start.15 = (s32[6]{0:T(128)S(1)}, s32[6]{0:T(128)}, u32[]{:S(2)}) copy-start(s32[6]{0:T(128)} %get-tuple-element.148) | copy-start | bytes 76
  820.1 141.3 %all-gather.33.cloned.1.call-start = ((), (), s32[]{:S(2)}) async-start(), calls=%async_computation.16 | async-start | bytes 2162688 | tf_op jit(solution)/shard_map/all_gather | solution.py:41
  884.7 143.3 %all-reduce.25.cloned.1.call-start = ((), (), s32[]{:S(2)}) async-start(), calls=%async_computation.6 | async-start | bytes 262144 | tf_op jit(solution)/shard_map/psum | solution.py:33
  965.2 208.2 %copy-start.8 = (bf16[128,256]{1,0:T(8,128)(2,1)S(1)}, bf16[128,256]{1,0:T(8,128)(2,1)}, u32[]{:S(2)}) copy-start(bf16[128,256]{1,0:T(8,128)(2,1)} %convolution_convert_fusion.9) | copy-start | bytes 196612
  965.2 141.5 %all-gather.35.cloned.1.call-start = ((), (), s32[]{:S(2)}) async-start(), calls=%async_computation.17 | async-start | bytes 2162688 | tf_op jit(solution)/shard_map/all_gather | solution.py:41
  1029.8 143.5 %all-reduce.27.cloned.1.call-start = ((), (), s32[]{:S(2)}) async-start(), calls=%async_computation.7 | async-start | bytes 262144 | tf_op jit(solution)/shard_map/psum | solution.py:33
  1110.5 207.8 %copy-start.7 = (bf16[128,256]{1,0:T(8,128)(2,1)S(1)}, bf16[128,256]{1,0:T(8,128)(2,1)}, u32[]{:S(2)}) copy-start(bf16[128,256]{1,0:T(8,128)(2,1)} %convolution_convert_fusion.10) | copy-start | bytes 196612
  1110.5 141.2 %all-gather.37.cloned.1.call-start = ((), (), s32[]{:S(2)}) async-start(), calls=%async_computation.18 | async-start | bytes 2162688 | tf_op jit(solution)/shard_map/all_gather | solution.py:41
  1175.1 143.2 %all-reduce.29.cloned.1.call-start = ((), (), s32[]{:S(2)}) async-start(), calls=%async_computation.8 | async-start | bytes 262144 | tf_op jit(solution)/shard_map/psum | solution.py:33
  1255.4 208.3 %copy-start.6 = (bf16[128,256]{1,0:T(8,128)(2,1)S(1)}, bf16[128,256]{1,0:T(8,128)(2,1)}, u32[]{:S(2)}) copy-start(bf16[128,256]{1,0:T(8,128)(2,1)} %convolution_convert_fusion.11) | copy-start | bytes 196612
  1255.5 209.4 %copy-start.4 = (bf16[128,256]{1,0:T(8,128)(2,1)S(1)}, bf16[128,256]{1,0:T(8,128)(2,1)}, u32[]{:S(2)}) copy-start(bf16[128,256]{1,0:T(8,128)(2,1)} %convolution_convert_fusion.2) | copy-start | bytes 196612
  1255.5 209.4 %copy-start.3 = (bf16[128,256]{1,0:T(8,128)(2,1)S(1)}, bf16[128,256]{1,0:T(8,128)(2,1)}, u32[]{:S(2)}) copy-start(bf16[128,256]{1,0:T(8,128)(2,1)} %convolution_convert_fusion.3) | copy-start | bytes 196612
  1255.5 141.6 %all-gather.39.cloned.1.call-start = ((), (), s32[]{:S(2)}) async-start(), calls=%async_computation.19 | async-start | bytes 2162688 | tf_op jit(solution)/shard_map/all_gather | solution.py:41
  1320.1 144.8 %copy-start.5 = (bf16[128,256]{1,0:T(8,128)(2,1)S(1)}, bf16[128,256]{1,0:T(8,128)(2,1)}, u32[]{:S(2)}) copy-start(bf16[128,256]{1,0:T(8,128)(2,1)} %convolution_convert_fusion.1) | copy-start | bytes 196612
  1320.1 144.9 %copy-start.2 = (bf16[128,256]{1,0:T(8,128)(2,1)S(1)}, bf16[128,256]{1,0:T(8,128)(2,1)}, u32[]{:S(2)}) copy-start(bf16[128,256]{1,0:T(8,128)(2,1)} %convolution_convert_fusion.4) | copy-start | bytes 196612
  1320.1 144.9 %copy-start.11 = (bf16[128,256]{1,0:T(8,128)(2,1)S(1)}, bf16[128,256]{1,0:T(8,128)(2,1)}, u32[]{:S(2)}) copy-start(bf16[128,256]{1,0:T(8,128)(2,1)} %convolution_convert_fusion.5) | copy-start | bytes 196612
  1320.1 143.6 %all-reduce.31.cloned.1.call-start = ((), (), s32[]{:S(2)}) async-start(), calls=%async_computation.9 | async-start | bytes 262144 | tf_op jit(solution)/shard_map/psum | solution.py:33
  1465.0 0.7 copy-start.14
Sparse Core Ops, SparseCore 0:
  9.9 79.6 all-gather.20
  93.7 62.6 all-reduce.12
  159.4 75.8 all-gather.22
  239.1 62.6 all-reduce.14
  304.3 75.8 all-gather.24
  384.1 62.6 all-reduce.16
  449.7 75.8 all-gather.26
  529.5 62.6 all-reduce.18
  594.8 75.8 all-gather.28
  674.6 62.6 all-reduce.20
  740.3 75.8 all-gather.30
  820.2 62.7 all-reduce.22
  885.6 75.8 all-gather.32
  965.3 62.6 all-reduce.24
  1030.9 75.8 all-gather.34
  1110.6 62.6 all-reduce.26
  1175.8 75.8 all-gather.36
  1255.6 62.6 all-reduce.28
  1321.2 75.8 all-gather.38
  1401.0 62.6 all-reduce.30
where the time goes:
time: 1470 us
  waiting for transfers between devices  1390 us (95%)
  matrix products  40.5 us (3%)
  local copies, waits for them, and re-layouts  18.7 us (1%)
    all_gather x10, waiting for transfers between devices, spread(): whole = lax.all_gather(solved[None], 'prow', axis=0, tiled=True)  760 us
    psum x10, waiting for transfers between devices, solve_level(): total = lax.psum(contract(picked, blocks), 'pcol')  628 us
  transfers between devices with their start and end apart: 20, of which 20 were waited for; matrix products, arithmetic and copies ran while one was open for 1% of the time, Pallas kernels for 0%

commit v1 on v0

--- a/solution.py
+++ b/solution.py
@@ -30,7 +30,8 @@
     width = lax.axis_size("prow")
     ncol = lax.axis_size("pcol")
     picked = pick_sources(sources, count, store, width, ncol)
-    total = lax.psum(contract(picked, blocks), "pcol")
+    piece_in = contract(picked, blocks)
+    total = jax.lax.all_gather(piece_in, "pcol").sum(axis=0)
     residual = (right.astype(jnp.float32) - total).astype(jnp.bfloat16)
     return apply_inverse(residual, inverse)
 

time: 1470 us -> 1100 us (0.75)
  waiting for transfers between devices: 1390 us -> 1010 us
    psum x10 -> x0, waiting for transfers between devices: 628 us -> none  [solve_level(): total = lax.psum(contract(picked, blocks), 'pcol')]
    all_gather x0 -> x10, waiting for transfers between devices: none -> 244 us  [solve_level(): total = jax.lax.all_gather(piece_in, 'pcol').sum(axis=0)]
where the time goes in v1:
time: 1100 us
  waiting for transfers between devices  1010 us (92%)
  matrix products  32.3 us (3%)
  other arithmetic  21.3 us (2%)
  local copies, waits for them, and re-layouts  19 us (2%)
  between operations  14.3 us (1%)
    all_gather x10, waiting for transfers between devices, spread(): whole = lax.all_gather(solved[None], 'prow', axis=0, tiled=True)  763 us
    all_gather x10, waiting for transfers between devices, solve_level(): total = jax.lax.all_gather(piece_in, 'pcol').sum(axis=0)  244 us
  transfers between devices with their start and end apart: 20, of which 20 were waited for; matrix products, arithmetic and copies ran while one was open for 1% of the time, Pallas kernels for 0%

profile of v1, /device:TPU:8, one launch (start us, length us, event | category | flops | bytes accessed | tf_op | source)
XLA Modules:
  0.0 1095.3 jit_solution(10023883318430683575)
XLA Ops:
  6.5 1.8 convolution_convert_fusion.11
  8.4 1.5 fusion.123
  10.6 1.4 fusion.106
  12.0 77.6 %all-gather.41.cloned.1.call-done = bf16[4096,256]{1,0:T(8,128)(2,1)} async-done(((bf16[128,256]{1,0:T(8,128)(2,1)}), bf16[4096,256]{1,0:T(8,128)(2,1)}) %all-gather.41.cloned.1.call-update) | async-done | bytes 2097168 | tf_op jit(solution)/shard_map/all_gather | solution.py:42
  91.3 2.2 convolution_bitcast_fusion.9
  93.6 24.4 %all-gather.43.cloned.1.call-done = f32[1024,256]{1,0:T(8,128)} async-done(((f32[128,256]{1,0:T(8,128)}), f32[1024,256]{1,0:T(8,128)}) %all-gather.43.cloned.1.call-update) | async-done | bytes 1048592 | tf_op jit(solution)/shard_map/all_gather | solution.py:34
  118.0 1.3 reduce_sum.100
  120.8 76.5 %all-gather.45.cloned.1.call-done = bf16[4096,256]{1,0:T(8,128)(2,1)} async-done(((bf16[128,256]{1,0:T(8,128)(2,1)}), bf16[4096,256]{1,0:T(8,128)(2,1)}) %all-gather.45.cloned.1.call-update) | async-done | bytes 2097168 | tf_op jit(solution)/shard_map/all_gather | solution.py:42
  198.8 2.2 convolution_bitcast_fusion.8
  201.1 24.4 %all-gather.47.cloned.1.call-done = f32[1024,256]{1,0:T(8,128)} async-done(((f32[128,256]{1,0:T(8,128)}), f32[1024,256]{1,0:T(8,128)}) %all-gather.47.cloned.1.call-update) | async-done | bytes 1048592 | tf_op jit(solution)/shard_map/all_gather | solution.py:34
  225.5 1.3 reduce_sum.102
  228.4 76.2 %all-gather.49.cloned.1.call-done = bf16[4096,256]{1,0:T(8,128)(2,1)} async-done(((bf16[128,256]{1,0:T(8,128)(2,1)}), bf16[4096,256]{1,0:T(8,128)(2,1)}) %all-gather.49.cloned.1.call-update) | async-done | bytes 2097168 | tf_op jit(solution)/shard_map/all_gather | solution.py:42
  306.2 2.2 convolution_bitcast_fusion.7
  308.4 24.4 %all-gather.51.cloned.1.call-done = f32[1024,256]{1,0:T(8,128)} async-done(((f32[128,256]{1,0:T(8,128)}), f32[1024,256]{1,0:T(8,128)}) %all-gather.51.cloned.1.call-update) | async-done | bytes 1048592 | tf_op jit(solution)/shard_map/all_gather | solution.py:34
  332.8 1.3 reduce_sum.104
  335.6 76.4 %all-gather.53.cloned.1.call-done = bf16[4096,256]{1,0:T(8,128)(2,1)} async-done(((bf16[128,256]{1,0:T(8,128)(2,1)}), bf16[4096,256]{1,0:T(8,128)(2,1)}) %all-gather.53.cloned.1.call-update) | async-done | bytes 2097168 | tf_op jit(solution)/shard_map/all_gather | solution.py:42
  413.6 2.2 convolution_bitcast_fusion.6
  415.9 24.4 %all-gather.55.cloned.1.call-done = f32[1024,256]{1,0:T(8,128)} async-done(((f32[128,256]{1,0:T(8,128)}), f32[1024,256]{1,0:T(8,128)}) %all-gather.55.cloned.1.call-update) | async-done | bytes 1048592 | tf_op jit(solution)/shard_map/all_gather | solution.py:34
  440.3 1.3 reduce_sum.106
  442.5 1.1 iota_compare_fusion.8
  443.6 76.0 %all-gather.57.cloned.1.call-done = bf16[4096,256]{1,0:T(8,128)(2,1)} async-done(((bf16[128,256]{1,0:T(8,128)(2,1)}), bf16[4096,256]{1,0:T(8,128)(2,1)}) %all-gather.57.cloned.1.call-update) | async-done | bytes 2097168 | tf_op jit(solution)/shard_map/all_gather | solution.py:42
  519.6 1.0 bitcast_dynamic-update-slice_fusion.4
  521.2 2.2 convolution_bitcast_fusion.5
  523.5 24.4 %all-gather.59.cloned.1.call-done = f32[1024,256]{1,0:T(8,128)} async-done(((f32[128,256]{1,0:T(8,128)}), f32[1024,256]{1,0:T(8,128)}) %all-gather.59.cloned.1.call-update) | async-done | bytes 1048592 | tf_op jit(solution)/shard_map/all_gather | solution.py:34
  547.9 1.3 reduce_sum.108
  549.2 1.8 convolution_convert_fusion.5
  552.4 75.4 %all-gather.61.cloned.1.call-done = bf16[4096,256]{1,0:T(8,128)(2,1)} async-done(((bf16[128,256]{1,0:T(8,128)(2,1)}), bf16[4096,256]{1,0:T(8,128)(2,1)}) %all-gather.61.cloned.1.call-update) | async-done | bytes 2097168 | tf_op jit(solution)/shard_map/all_gather | solution.py:42
  629.5 2.2 convolution_bitcast_fusion.4
  631.8 24.4 %all-gather.63.cloned.1.call-done = f32[1024,256]{1,0:T(8,128)} async-done(((f32[128,256]{1,0:T(8,128)}), f32[1024,256]{1,0:T(8,128)}) %all-gather.63.cloned.1.call-update) | async-done | bytes 1048592 | tf_op jit(solution)/shard_map/all_gather | solution.py:34
  656.2 1.3 reduce_sum.110
  659.1 76.3 %all-gather.65.cloned.1.call-done = bf16[4096,256]{1,0:T(8,128)(2,1)} async-done(((bf16[128,256]{1,0:T(8,128)(2,1)}), bf16[4096,256]{1,0:T(8,128)(2,1)}) %all-gather.65.cloned.1.call-update) | async-done | bytes 2097168 | tf_op jit(solution)/shard_map/all_gather | solution.py:42
  735.5 1.0 bitcast_dynamic-update-slice_fusion.3
  737.1 2.2 convolution_bitcast_fusion.3
  739.3 24.4 %all-gather.67.cloned.1.call-done = f32[1024,256]{1,0:T(8,128)} async-done(((f32[128,256]{1,0:T(8,128)}), f32[1024,256]{1,0:T(8,128)}) %all-gather.67.cloned.1.call-update) | async-done | bytes 1048592 | tf_op jit(solution)/shard_map/all_gather | solution.py:34
  763.7 1.3 reduce_sum.111
  766.6 76.2 %all-gather.69.cloned.1.call-done = bf16[4096,256]{1,0:T(8,128)(2,1)} async-done(((bf16[128,256]{1,0:T(8,128)(2,1)}), bf16[4096,256]{1,0:T(8,128)(2,1)}) %all-gather.69.cloned.1.call-update) | async-done | bytes 2097168 | tf_op jit(solution)/shard_map/all_gather | solution.py:42
  842.9 1.0 bitcast_dynamic-update-slice_fusion.2
  844.4 2.2 convolution_bitcast_fusion.2
  846.7 24.4 %all-gather.71.cloned.1.call-done = f32[1024,256]{1,0:T(8,128)} async-done(((f32[128,256]{1,0:T(8,128)}), f32[1024,256]{1,0:T(8,128)}) %all-gather.71.cloned.1.call-update) | async-done | bytes 1048592 | tf_op jit(solution)/shard_map/all_gather | solution.py:34
  871.1 1.3 reduce_sum.112
  873.9 76.3 %all-gather.73.cloned.1.call-done = bf16[4096,256]{1,0:T(8,128)(2,1)} async-done(((bf16[128,256]{1,0:T(8,128)(2,1)}), bf16[4096,256]{1,0:T(8,128)(2,1)}) %all-gather.73.cloned.1.call-update) | async-done | bytes 2097168 | tf_op jit(solution)/shard_map/all_gather | solution.py:42
  951.8 2.2 convolution_bitcast_fusion.1
  954.1 24.4 %all-gather.75.cloned.1.call-done = f32[1024,256]{1,0:T(8,128)} async-done(((f32[128,256]{1,0:T(8,128)}), f32[1024,256]{1,0:T(8,128)}) %all-gather.75.cloned.1.call-update) | async-done | bytes 1048592 | tf_op jit(solution)/shard_map/all_gather | solution.py:34
  978.4 1.3 reduce_sum.113
  981.3 76.4 %all-gather.77.cloned.1.call-done = bf16[4096,256]{1,0:T(8,128)(2,1)} async-done(((bf16[128,256]{1,0:T(8,128)(2,1)}), bf16[4096,256]{1,0:T(8,128)(2,1)}) %all-gather.77.cloned.1.call-update) | async-done | bytes 2097168 | tf_op jit(solution)/shard_map/all_gather | solution.py:42
  1059.4 2.2 convolution_bitcast_fusion
  1061.6 24.4 %all-gather.79.cloned.1.call-done = f32[1024,256]{1,0:T(8,128)} async-done(((f32[128,256]{1,0:T(8,128)}), f32[1024,256]{1,0:T(8,128)}) %all-gather.79.cloned.1.call-update) | async-done | bytes 1048592 | tf_op jit(solution)/shard_map/all_gather | solution.py:34
  1086.0 1.3 reduce_sum.114
  (129 shorter events, 28.1 us)
Async XLA Ops:
  6.5 83.1 %all-gather.41.cloned.1.call-start = ((), (), s32[]{:S(2)}) async-start(), calls=%async_computation | async-start | bytes 2162688 | tf_op jit(solution)/shard_map/all_gather | solution.py:42
  8.3 109.7 %all-gather.43.cloned.1.call-start = ((), (), s32[]{:S(2)}) async-start(), calls=%async_computation.1 | async-start | bytes 1179648 | tf_op jit(solution)/shard_map/all_gather | solution.py:34
  90.7 28.6 %copy-start.1 = (bf16[1,6,256,256]{3,2,1,0:T(8,128)(2,1)S(1)}, bf16[1,6,256,256]{3,2,1,0:T(8,128)(2,1)}, u32[]{:S(2)}) copy-start(bf16[1,6,256,256]{3,2,1,0:T(8,128)(2,1)} %param.30) | copy-start | bytes 2359300
  90.8 28.5 %copy-start.12 = (bf16[1,6,128,256]{3,2,1,0:T(8,128)(2,1)S(1)}, bf16[1,6,128,256]{3,2,1,0:T(8,128)(2,1)}, u32[]{:S(2)}) copy-start(bf16[1,6,128,256]{3,2,1,0:T(8,128)(2,1)} %param.29) | copy-start | bytes 1179652
  93.6 103.7 %all-gather.45.cloned.1.call-start = ((), (), s32[]{:S(2)}) async-start(), calls=%async_computation.2 | async-start | bytes 2162688 | tf_op jit(solution)/shard_map/all_gather | solution.py:42
  120.2 105.3 %all-gather.47.cloned.1.call-start = ((), (), s32[]{:S(2)}) async-start(), calls=%async_computation.3 | async-start | bytes 1179648 | tf_op jit(solution)/shard_map/all_gather | solution.py:34
  201.1 103.6 %all-gather.49.cloned.1.call-start = ((), (), s32[]{:S(2)}) async-start(), calls=%async_computation.4 | async-start | bytes 2162688 | tf_op jit(solution)/shard_map/all_gather | solution.py:42
  227.6 105.2 %all-gather.51.cloned.1.call-start = ((), (), s32[]{:S(2)}) async-start(), calls=%async_computation.5 | async-start | bytes 1179648 | tf_op jit(solution)/shard_map/all_gather | solution.py:34
  308.4 103.7 %all-gather.53.cloned.1.call-start = ((), (), s32[]{:S(2)}) async-start(), calls=%async_computation.6 | async-start | bytes 2162688 | tf_op jit(solution)/shard_map/all_gather | solution.py:42
  335.0 105.3 %all-gather.55.cloned.1.call-start = ((), (), s32[]{:S(2)}) async-start(), calls=%async_computation.7 | async-start | bytes 1179648 | tf_op jit(solution)/shard_map/all_gather | solution.py:34
  415.9 103.7 %all-gather.57.cloned.1.call-start = ((), (), s32[]{:S(2)}) async-start(), calls=%async_computation.8 | async-start | bytes 2162688 | tf_op jit(solution)/shard_map/all_gather | solution.py:42
  442.4 105.4 %all-gather.59.cloned.1.call-start = ((), (), s32[]{:S(2)}) async-start(), calls=%async_computation.9 | async-start | bytes 1179648 | tf_op jit(solution)/shard_map/all_gather | solution.py:34
  519.6 29.6 %copy-start = (bf16[1,6,256,256]{3,2,1,0:T(8,128)(2,1)S(1)}, bf16[1,6,256,256]{3,2,1,0:T(8,128)(2,1)}, u32[]{:S(2)}) copy-start(bf16[1,6,256,256]{3,2,1,0:T(8,128)(2,1)} %param.31) | copy-start | bytes 2359300
  520.6 30.4 %copy-start.13 = (s32[1,5,1]{1,2,0:T(1,128)S(1)}, s32[1,5,1]{1,2,0:T(1,128)}, u32[]{:S(2)}) copy-start(s32[1,5,1]{1,2,0:T(1,128)} %param.37) | copy-start | bytes 64
  521.2 31.2 %copy-start.17 = (s32[6]{0:T(128)S(1)}, s32[6]{0:T(128)}, u32[]{:S(2)}) copy-start(s32[6]{0:T(128)} %get-tuple-element.146) | copy-start | bytes 76
  523.4 104.4 %all-gather.61.cloned.1.call-start = ((), (), s32[]{:S(2)}) async-start(), calls=%async_computation.10 | async-start | bytes 2162688 | tf_op jit(solution)/shard_map/all_gather | solution.py:42
  551.0 105.2 %all-gather.63.cloned.1.call-start = ((), (), s32[]{:S(2)}) async-start(), calls=%async_computation.11 | async-start | bytes 1179648 | tf_op jit(solution)/shard_map/all_gather | solution.py:34
  628.9 28.6 %copy-start.10 = (bf16[128,256]{1,0:T(8,128)(2,1)S(1)}, bf16[128,256]{1,0:T(8,128)(2,1)}, u32[]{:S(2)}) copy-start(bf16[128,256]{1,0:T(8,128)(2,1)} %convolution_convert_fusion.7) | copy-start | bytes 196612
  629.0 30.1 %copy-start.16 = (s32[6]{0:T(128)S(1)}, s32[6]{0:T(128)}, u32[]{:S(2)}) copy-start(s32[6]{0:T(128)} %get-tuple-element.147) | copy-start | bytes 76
  631.8 103.7 %all-gather.65.cloned.1.call-start = ((), (), s32[]{:S(2)}) async-start(), calls=%async_computation.12 | async-start | bytes 2162688 | tf_op jit(solution)/shard_map/all_gather | solution.py:42
  658.4 105.4 %all-gather.67.cloned.1.call-start = ((), (), s32[]{:S(2)}) async-start(), calls=%async_computation.13 | async-start | bytes 1179648 | tf_op jit(solution)/shard_map/all_gather | solution.py:34
  735.5 29.5 %copy-start.9 = (bf16[128,256]{1,0:T(8,128)(2,1)S(1)}, bf16[128,256]{1,0:T(8,128)(2,1)}, u32[]{:S(2)}) copy-start(bf16[128,256]{1,0:T(8,128)(2,1)} %convolution_convert_fusion.8) | copy-start | bytes 196612
  736.5 30.1 %copy-start.15 = (s32[6]{0:T(128)S(1)}, s32[6]{0:T(128)}, u32[]{:S(2)}) copy-start(s32[6]{0:T(128)} %get-tuple-element.148) | copy-start | bytes 76
  739.3 103.6 %all-gather.69.cloned.1.call-start = ((), (), s32[]{:S(2)}) async-start(), calls=%async_computation.14 | async-start | bytes 2162688 | tf_op jit(solution)/shard_map/all_gather | solution.py:42
  765.9 105.2 %all-gather.71.cloned.1.call-start = ((), (), s32[]{:S(2)}) async-start(), calls=%async_computation.15 | async-start | bytes 1179648 | tf_op jit(solution)/shard_map/all_gather | solution.py:34
  842.8 29.5 %copy-start.8 = (bf16[128,256]{1,0:T(8,128)(2,1)S(1)}, bf16[128,256]{1,0:T(8,128)(2,1)}, u32[]{:S(2)}) copy-start(bf16[128,256]{1,0:T(8,128)(2,1)} %convolution_convert_fusion.9) | copy-start | bytes 196612
  846.7 103.6 %all-gather.73.cloned.1.call-start = ((), (), s32[]{:S(2)}) async-start(), calls=%async_computation.16 | async-start | bytes 2162688 | tf_op jit(solution)/shard_map/all_gather | solution.py:42
  873.2 105.2 %all-gather.75.cloned.1.call-start = ((), (), s32[]{:S(2)}) async-start(), calls=%async_computation.17 | async-start | bytes 1179648 | tf_op jit(solution)/shard_map/all_gather | solution.py:34
  950.2 29.5 %copy-start.7 = (bf16[128,256]{1,0:T(8,128)(2,1)S(1)}, bf16[128,256]{1,0:T(8,128)(2,1)}, u32[]{:S(2)}) copy-start(bf16[128,256]{1,0:T(8,128)(2,1)} %convolution_convert_fusion.10) | copy-start | bytes 196612
  954.0 103.7 %all-gather.77.cloned.1.call-start = ((), (), s32[]{:S(2)}) async-start(), calls=%async_computation.18 | async-start | bytes 2162688 | tf_op jit(solution)/shard_map/all_gather | solution.py:42
  980.6 105.4 %all-gather.79.cloned.1.call-start = ((), (), s32[]{:S(2)}) async-start(), calls=%async_computation.19 | async-start | bytes 1179648 | tf_op jit(solution)/shard_map/all_gather | solution.py:34
  1057.7 29.6 %copy-start.6 = (bf16[128,256]{1,0:T(8,128)(2,1)S(1)}, bf16[128,256]{1,0:T(8,128)(2,1)}, u32[]{:S(2)}) copy-start(bf16[128,256]{1,0:T(8,128)(2,1)} %convolution_convert_fusion.11) | copy-start | bytes 196612
  1058.7 28.8 %copy-start.5 = (bf16[128,256]{1,0:T(8,128)(2,1)S(1)}, bf16[128,256]{1,0:T(8,128)(2,1)}, u32[]{:S(2)}) copy-start(bf16[128,256]{1,0:T(8,128)(2,1)} %convolution_convert_fusion.1) | copy-start | bytes 196612
  1058.7 28.8 %copy-start.4 = (bf16[128,256]{1,0:T(8,128)(2,1)S(1)}, bf16[128,256]{1,0:T(8,128)(2,1)}, u32[]{:S(2)}) copy-start(bf16[128,256]{1,0:T(8,128)(2,1)} %convolution_convert_fusion.2) | copy-start | bytes 196612
  1058.7 28.9 %copy-start.3 = (bf16[128,256]{1,0:T(8,128)(2,1)S(1)}, bf16[128,256]{1,0:T(8,128)(2,1)}, u32[]{:S(2)}) copy-start(bf16[128,256]{1,0:T(8,128)(2,1)} %convolution_convert_fusion.3) | copy-start | bytes 196612
  1059.3 28.3 %copy-start.2 = (bf16[128,256]{1,0:T(8,128)(2,1)S(1)}, bf16[128,256]{1,0:T(8,128)(2,1)}, u32[]{:S(2)}) copy-start(bf16[128,256]{1,0:T(8,128)(2,1)} %convolution_convert_fusion.4) | copy-start | bytes 196612
  1059.3 28.3 %copy-start.11 = (bf16[128,256]{1,0:T(8,128)(2,1)S(1)}, bf16[128,256]{1,0:T(8,128)(2,1)}, u32[]{:S(2)}) copy-start(bf16[128,256]{1,0:T(8,128)(2,1)} %convolution_convert_fusion.5) | copy-start | bytes 196612
  1087.7 0.7 copy-start.14
Sparse Core Ops, SparseCore 0:
  9.9 79.6 all-gather.40
  93.7 24.2 all-gather.42
  120.6 76.6 all-gather.44
  201.2 24.2 all-gather.46
  227.9 76.6 all-gather.48
  308.5 24.2 all-gather.50
  335.4 76.6 all-gather.52
  416.0 24.2 all-gather.54
  442.9 76.6 all-gather.56
  523.6 24.2 all-gather.58
  551.1 76.6 all-gather.60
  631.9 24.2 all-gather.62
  658.8 76.6 all-gather.64
  739.4 24.2 all-gather.66
  766.2 76.6 all-gather.68
  846.8 24.2 all-gather.70
  873.5 76.6 all-gather.72
  954.1 24.2 all-gather.74
  981.0 76.6 all-gather.76
  1061.7 24.2 all-gather.78
